TPU v7x, 32 devices: a whole 2x2x4 slice. The times are simulated.
32 devices in a mesh: group: 2 (over x), engine: 4 (over y, core), chan: 4 (over z).
Axes of the slice: x: 2, y: 2, z: 4, core: 2. Of those that a mesh axis runs over, the one named last changes fastest.
Arguments:
- mr_qkv: bfloat16 [2, 3, 128, 8192], P(None, None, ('group', 'engine'), 'chan'), parts along dimension 2, may hold values from -6 to 6
- li_qkv: bfloat16 [2, 3, 128, 8192], P(None, None, ('group', 'engine'), 'chan'), parts along dimension 2, may hold values from -6 to 6
- conv_tails: bfloat16 [128, 127, 8192], P(('group', 'engine'), None, 'chan'), parts along dimension 0, may hold values from -6 to 6
- modal_states: float32 [128, 16, 8192], P(('group', 'engine'), None, 'chan'), parts along dimension 0, may hold values from -12 to 12
- source: int32 [128], P('group'), parts along dimension 0, may hold values from 0 to 63, as said below
- remaining: int32 [128], P(('group', 'engine')), parts along dimension 0, may hold values from 0 to 3
- mr_filter: bfloat16 [128, 8192], P(None, 'chan'), may hold values from -0.5 to 0.5
- li_decay: float32 [16, 8192], P(None, 'chan'), may hold values from 0.5 to 0.999
- li_residue: float32 [16, 8192], P(None, 'chan'), may hold values from -1.5 to 1.5
- mr_panels: bfloat16 [8, 8192, 512], P('engine', 'chan'), may hold values from -0.046875 to 0.046875
- li_panels: bfloat16 [8, 8192, 512], P('engine', 'chan'), may hold values from -0.046875 to 0.046875
- panel_slot: int32 [8], replicated, may hold values from 0 to 7, each once
Outputs:
- mixed: bfloat16 [2, 128, 4096], P(None, ('group', 'engine'), 'chan'), parts along dimension 1
- new_tails: bfloat16 [128, 127, 8192], P(('group', 'engine'), None, 'chan'), parts along dimension 0
- new_states: float32 [128, 16, 8192], P(('group', 'engine'), None, 'chan'), parts along dimension 0
There are 2 independent parts, one for each index of `group`. A program takes and returns all parts, laid end to end along the dimension named above; an argument that names none is the same for every part. Nothing has to cross between parts.
Inputs may be any that keep to these rules, and one draw needn't show every extreme that they name: `source`: A permutation of the old slots. Each engine's 16 new slots hold exactly 2 rollouts from each of 3 other engines and 10 rollouts from its own old slots; engine e takes from the engines e - d mod 4 for 3 distances d that are the same for every engine, so every engine also gives exactly 2 rollouts to each of 3 others.
All inputs are finite; a program needn't handle non-finite values.
Results may differ from a plain program's by a relative error of at most 0.008.
Values may be sent and summed in bfloat16 or wider, within the bound.
No kernel may reach another device: no remote copies, remote signals or barrier semaphores. Data moves between devices by JAX's collectives and lax.ppermute only.
A program may use at most 192 MiB of HBM per device.

v0:
```python
import jax
import jax.numpy as jnp
from jax import lax
from jax.sharding import PartitionSpec as P

CAP = 2


def body(
    mr_qkv,
    li_qkv,
    conv_tails,
    modal_states,
    source,
    remaining,
    mr_filter,
    li_decay,
    li_residue,
    mr_panels,
    li_panels,
    panel_slot,
):
    engines = lax.axis_size("engine")
    me = lax.axis_index("engine")
    rows = conv_tails.shape[0]
    tail_len = conv_tails.shape[1]
    width = conv_tails.shape[2]
    panel_cols = mr_panels.shape[2]
    panel_count = panel_slot.shape[0]
    owners = source.reshape(engines, rows)
    engine_ids = jnp.arange(engines, dtype=jnp.int32)
    from_me = (owners // rows == me) & (engine_ids[:, None] != me)
    order_rank = jnp.cumsum(from_me.astype(jnp.int32), axis=1) - 1
    place_ids = jnp.arange(CAP, dtype=jnp.int32)
    picks = from_me[:, :, None] & (order_rank[:, :, None] == place_ids[None, None, :])
    send_index = jnp.sum(picks.astype(jnp.int32) * (owners % rows)[:, :, None], axis=1)
    send_tails = conv_tails[send_index.reshape(-1)].reshape(engines, CAP, tail_len, width)
    send_states = modal_states[send_index.reshape(-1)].reshape(
        engines, CAP, modal_states.shape[1], width
    )
    got_tails = lax.all_to_all(send_tails, "engine", split_axis=0, concat_axis=0, tiled=True)
    got_states = lax.all_to_all(send_states, "engine", split_axis=0, concat_axis=0, tiled=True)
    mine = lax.dynamic_slice_in_dim(source, me * rows, rows)
    src_engine = mine // rows
    src_local = mine % rows
    row_ids = jnp.arange(rows, dtype=jnp.int32)
    earlier = (src_engine[:, None] == src_engine[None, :]) & (row_ids[None, :] < row_ids[:, None])
    arrive_rank = jnp.sum(earlier.astype(jnp.int32), axis=1)
    arrive_index = jnp.clip(src_engine * CAP + arrive_rank, 0, engines * CAP - 1)
    stays = src_engine == me
    tails = jnp.where(
        stays[:, None, None],
        conv_tails[src_local],
        got_tails.reshape(engines * CAP, tail_len, width)[arrive_index],
    )
    states = jnp.where(
        stays[:, None, None],
        modal_states[src_local],
        got_states.reshape(engines * CAP, got_states.shape[2], width)[arrive_index],
    )
    filt = mr_filter.astype(jnp.float32)
    part_first = jnp.einsum("rtc,tc->rc", tails, mr_filter[1:], preferred_element_type=jnp.float32)
    part_second = jnp.einsum(
        "rtc,tc->rc", tails[:, : tail_len - 1], mr_filter[2:], preferred_element_type=jnp.float32
    )
    zmr_first = (mr_qkv[0, 1].astype(jnp.float32) * mr_qkv[0, 2].astype(jnp.float32)).astype(
        jnp.bfloat16
    )
    zmr_second = (mr_qkv[1, 1].astype(jnp.float32) * mr_qkv[1, 2].astype(jnp.float32)).astype(
        jnp.bfloat16
    )
    new_tails = jnp.concatenate(
        [zmr_second[:, None, :], zmr_first[:, None, :], tails[:, : tail_len - 2]], axis=1
    )
    zmr0 = zmr_first.astype(jnp.float32)
    zmr1 = zmr_second.astype(jnp.float32)
    conv0 = filt[0] * zmr0 + part_first
    conv1 = filt[0] * zmr1 + filt[1] * zmr0 + part_second
    ymr0 = (mr_qkv[0, 0].astype(jnp.float32) * conv0).astype(jnp.bfloat16)
    ymr1 = (mr_qkv[1, 0].astype(jnp.float32) * conv1).astype(jnp.bfloat16)
    zli0 = (
        (li_qkv[0, 1].astype(jnp.float32) * li_qkv[0, 2].astype(jnp.float32))
        .astype(jnp.bfloat16)
        .astype(jnp.float32)
    )
    zli1 = (
        (li_qkv[1, 1].astype(jnp.float32) * li_qkv[1, 2].astype(jnp.float32))
        .astype(jnp.bfloat16)
        .astype(jnp.float32)
    )
    states1 = li_decay[None] * states + zli0[:, None, :]
    yli0 = (li_qkv[0, 0].astype(jnp.float32) * jnp.sum(li_residue[None] * states1, axis=1)).astype(
        jnp.bfloat16
    )
    states2 = li_decay[None] * states1 + zli1[:, None, :]
    yli1 = (li_qkv[1, 0].astype(jnp.float32) * jnp.sum(li_residue[None] * states2, axis=1)).astype(
        jnp.bfloat16
    )
    mr_rows = jnp.stack([ymr0, ymr1])
    li_rows = jnp.stack([yli0, yli1])
    mr_piece = lax.all_gather(mr_panels, "engine", axis=0, tiled=True)
    li_piece = lax.all_gather(li_panels, "engine", axis=0, tiled=True)
    upper = jnp.einsum("srd,gdc->srgc", mr_rows, mr_piece, preferred_element_type=jnp.float32)
    lower = jnp.einsum("srd,gdc->srgc", li_rows, li_piece, preferred_element_type=jnp.float32)
    sectioned = upper + lower
    partial_value = jnp.take(sectioned, panel_slot, axis=2).reshape(
        2, rows, panel_count * panel_cols
    )
    summed = lax.psum_scatter(partial_value, "chan", scatter_dimension=2, tiled=True)
    steps_ids = jnp.arange(2, dtype=jnp.int32)
    active = (remaining[None, :] > steps_ids[:, None]).astype(jnp.float32)
    mixed = (summed * active[:, :, None]).astype(jnp.bfloat16)
    return (mixed, new_tails, states2)


def solution(mesh):
    return jax.shard_map(
        body,
        mesh=mesh,
        in_specs=(
            P(None, None, ("group", "engine"), "chan"),
            P(None, None, ("group", "engine"), "chan"),
            P(("group", "engine"), None, "chan"),
            P(("group", "engine"), None, "chan"),
            P("group"),
            P(("group", "engine")),
            P(None, "chan"),
            P(None, "chan"),
            P(None, "chan"),
            P("engine", "chan", None),
            P("engine", "chan", None),
            P(),
        ),
        out_specs=(
            P(None, ("group", "engine"), "chan"),
            P(("group", "engine"), None, "chan"),
            P(("group", "engine"), None, "chan"),
        ),
        check_vma=False,
    )
```

profile of v0, /device:TPU:0, one launch (start us, length us, event | category | flops | bytes accessed | tf_op | source)
XLA Modules:
  0.0 315.2 jit_solution(9834262589492569166)
XLA Ops:
  7.2 0.0 all-gather.5.cloned.1.call-start
  7.2 0.7 all-gather.5.cloned.1.call-update
  7.9 0.0 all-gather.3.cloned.1.call-start
  8.0 0.7 all-gather.3.cloned.1.call-update
  8.7 0.1 reshape.363
  8.8 0.1 fusion.36
  8.9 0.2 reduce_window_sum.11
  9.1 0.1 select_reduce_fusion
  9.2 0.1 copy.22
  9.3 0.1 reshape.364
  9.4 1.6 gather_fusion.4
  11.0 4.2 %all-to-all-start.1 = ((f32[4,2,16,2048]{3,2,1,0:T(8,128)}), f32[4,2,16,2048]{3,2,1,0:T(8,128)S(1)}, u32[]{:S(2)}, u32[]{:S(2)}) async-start(f32[4,2,16,2048]{3,2,1,0:T(8,128)} %bitcast.94), calls=%async_computation.1 | async-start | bytes 2097152 | tf_op jit(solution)/shard_map/all_to_all | solution.py:42
  15.2 0.7 broadcast_compare_fusion.1
  15.9 0.2 convert_reduce_fusion
  16.1 13.2 %gather_fusion.1 = bf16[8,127,2048]{2,0,1:T(8,128)(2,1)} fusion(bf16[16,127,2048]{2,0,1:T(8,128)(2,1)} %param.14, s32[1024]{0:T(1024)S(1)} %pad_clamp_fusion.2), kind=kCustom, calls=%fused_computation.1 | custom fusion | bytes 8323104 | tf_op jit(solution)/shard_map/gather | solution.py:37
  29.3 9.3 %reshape.365 = bf16[4,2,127,2048]{3,1,0,2:T(2,128)(2,1)} reshape(bf16[8,127,2048]{2,0,1:T(8,128)(2,1)} %gather_fusion.1) | data formatting | bytes 8323072 | tf_op jit(solution)/shard_map/reshape | solution.py:37
  38.6 7.0 %copy.23 = bf16[4,2,127,2048]{3,1,2,0:T(2,128)(2,1)} copy(bf16[4,2,127,2048]{3,1,0,2:T(2,128)(2,1)} %reshape.365) | data formatting | bytes 8323072 | tf_op jit(solution)/shard_map/reshape | solution.py:37
  45.6 0.6 pad_clamp_fusion.1
  46.2 0.1 broadcast_bitcast_fusion
  46.3 5.1 %all-to-all-start = ((bf16[4,2,127,2048]{3,1,2,0:T(2,128)(2,1)}), bf16[4,2,127,2048]{3,1,2,0:T(2,128)(2,1)}, u32[]{:S(2)}, u32[]{:S(2)}) async-start(bf16[4,2,127,2048]{3,1,2,0:T(2,128)(2,1)} %copy.23), calls=%async_computation | async-start | bytes 8323072 | tf_op jit(solution)/shard_map/all_to_all | solution.py:41
  51.3 0.0 reduce-scatter.2.cloned.1.call-start
  51.4 18.6 %gather_fusion = bf16[16,127,2048]{2,0,1:T(8,128)(2,1)} fusion(bf16[16,127,2048]{2,0,1:T(8,128)(2,1)} %param.14, s32[1024]{0:T(1024)S(1)} %pad_clamp_fusion.3), kind=kCustom, calls=%fused_computation | custom fusion | bytes 16646208 | tf_op jit(solution)/shard_map/gather | solution.py:53
  70.0 2.0 gather_fusion.3
  72.0 0.6 copy.46
  72.6 0.6 pad_clamp_fusion
  73.2 0.8 fusion.38
  74.1 1.0 fusion.23
  75.0 2.2 bitcast_convert_fusion.1
  77.2 2.2 bitcast_convert_fusion
  79.4 2.2 gather_fusion.5
  81.6 4.0 %multiply_reduce_fusion.3 = (f32[16,2048]{1,0:T(8,128)S(1)}, f32[16,2048]{1,0:T(8,128)S(1)}, f32[16,16,2048]{2,1,0:T(8,128)}) fusion(f32[16,2048]{1,0:T(8,128)S(1)} %copy-done.7, f32[16,2048]{1,0:T(8,128)S(1)} %get-tuple-element.22, f32[16,16,2048]{2,1,0:T(8,128)S(1)} %copy-done.3, f32[16,16,2048]{2,1,0:T(8,128)} %gather_fusion.5, ...), kind=kLoop, calls=%fused_computation.18 | loop fusion | flops 4653056 | bytes 7077904 | tf_op jit(solution)/shard_map/reduce_sum | solution.py:92
  85.6 0.9 fusion.19
  86.5 58.1 %all-to-all-done = bf16[4,2,127,2048]{3,1,2,0:T(2,128)(2,1)} async-done(((bf16[4,2,127,2048]{3,1,2,0:T(2,128)(2,1)}), bf16[4,2,127,2048]{3,1,2,0:T(2,128)(2,1)}, u32[]{:S(2)}, u32[]{:S(2)}) %all-to-all-start) | async-done | bytes 4161568 | tf_op jit(solution)/shard_map/all_to_all | solution.py:41
  144.6 6.0 %copy.24 = bf16[4,2,127,2048]{3,2,1,0:T(8,128)(2,1)} copy(bf16[4,2,127,2048]{3,1,2,0:T(2,128)(2,1)} %all-to-all-done) | data formatting | bytes 8323072 | tf_op jit(solution)/shard_map/all_to_all | solution.py:41
  150.6 7.1 %gather_fusion.2 = bf16[16,127,2048]{2,1,0:T(8,128)(2,1)} fusion(bf16[8,127,2048]{2,1,0:T(8,128)(2,1)} %bitcast.92, s32[1024]{0:T(1024)} %pad_clamp_fusion.1), kind=kCustom, calls=%fused_computation.2 | custom fusion | bytes 16646208 | tf_op jit(solution)/shard_map/gather | solution.py:54
  157.8 11.0 %multiply_reduce_fusion = (f32[2048,16]{0,1:T(8,128)S(1)}, bf16[16,127,2048]{2,0,1:T(8,128)(2,1)S(1)}) fusion(f32[2048,127]{0,1:T(8,128)S(1)} %copy-done.5, bf16[16,127,2048]{2,0,1:T(8,128)(2,1)} %gather_fusion, bf16[16,127,2048]{2,1,0:T(8,128)(2,1)} %gather_fusion.2, pred[16]{0:T(512)(128)(4,1)S(1)} %copy-done.9), kind=kLoop, calls=%fused_computation.11 | loop fusion | flops 16613376 | bytes 26140688 | tf_op jit(solution)/shard_map/rtc,tc->rc/dot_general | solution.py:62
  168.8 3.3 %copy-done.2 = bf16[16,127,2048]{2,0,1:T(8,128)(2,1)} copy-done((bf16[16,127,2048]{2,0,1:T(8,128)(2,1)}, bf16[16,127,2048]{2,0,1:T(8,128)(2,1)S(1)}, u32[]{:S(2)}) %copy-start.2) | copy-done | bytes 8323096
  172.1 2.4 multiply_reduce_fusion.1
  174.5 0.1 fusion.25
  174.7 11.4 %fusion = f32[2,16,8,512]{3,1,2,0:T(8,128)S(1)} fusion(bf16[8,2048,512]{2,1,0:T(8,128)(2,1)} %all-gather.5.cloned.1.call-done, bf16[1,16,2048]{2,1,0:T(8,128)(2,1)S(1)} %get-tuple-element.20, bf16[1,16,2048]{2,1,0:T(8,128)(2,1)S(1)} %get-tuple-element.19), kind=kOutput, calls=%fused_computation.7 | convolution fusion | flops 537133056 | bytes 17432576 | tf_op jit(solution)/shard_map/srd,gdc->srgc/dot_general | solution.py:104
  186.1 88.8 %all-gather.3.cloned.1.call-done = bf16[8,2048,512]{2,1,0:T(8,128)(2,1)} async-done(((bf16[2,2048,512]{2,1,0:T(8,128)(2,1)}), bf16[8,2048,512]{2,1,0:T(8,128)(2,1)}) %all-gather.3.cloned.1.call-update) | async-done | bytes 16777232 | tf_op jit(solution)/shard_map/all_gather | solution.py:101
  274.9 8.7 %fusion.4 = f32[2,16,8,512]{3,1,2,0:T(8,128)S(1)} fusion(f32[2,16,8,512]{3,1,2,0:T(8,128)S(1)} %fusion, bf16[8,2048,512]{2,1,0:T(8,128)(2,1)} %all-gather.3.cloned.1.call-done, bf16[1,16,2048]{2,1,0:T(8,128)(2,1)S(1)} %get-tuple-element.16, bf16[1,16,2048]{2,1,0:T(8,128)(2,1)S(1)} %get-tuple-element.15), kind=kOutput, calls=%fused_computation.20 | convolution fusion | flops 537264128 | bytes 17956864 | tf_op jit(solution)/shard_map/srd,gdc->srgc/dot_general | solution.py:103
  283.6 0.7 gather_fusion.6
  284.3 0.9 broadcast_select_fusion
  285.3 8.1 %slice.90 = bf16[16,125,2048]{2,0,1:T(8,128)(2,1)} slice(bf16[16,127,2048]{2,0,1:T(8,128)(2,1)} %copy-done.2), slice={[0:16], [0:125], [0:2048]} | slice | bytes 16384000 | tf_op jit(solution)/shard_map/slice | solution.py:73
  293.4 7.2 %pad_maximum_fusion = bf16[16,127,2048]{2,0,1:T(8,128)(2,1)} fusion(bf16[16,125,2048]{2,0,1:T(8,128)(2,1)} %slice.90, bf16[16,1,2048]{2,0,1:T(8,128)(2,1)S(1)} %get-tuple-element.18, bf16[16,1,2048]{2,0,1:T(8,128)(2,1)S(1)} %get-tuple-element.17), kind=kLoop, calls=%fused_computation.13 | loop fusion | flops 8323072 | bytes 16646144 | tf_op jit(solution)/shard_map/concatenate | solution.py:72
  300.6 6.4 %reduce-scatter.2.cloned.1.call-done = f32[2,16,1024]{2,1,0:T(8,128)} async-done(((f32[2,16,4096]{2,1,0:T(8,128)}), f32[2,16,1024]{2,1,0:T(8,128)}) %reduce-scatter.2.cloned.1.call-update) | async-done | bytes 131088 | tf_op jit(solution)/shard_map/reduce_scatter | solution.py:109
  307.1 1.6 multiply_convert_fusion
  (40 shorter events, 0.2 us)
Async XLA Ops:
  7.2 2.2 copy-start
  7.2 1.5 copy-start.10
  7.2 167.5 %all-gather.5.cloned.1.call-start = ((), (), s32[]{:S(2)}) async-start(), calls=%async_computation.4 | async-start | bytes 20971520 | tf_op jit(solution)/shard_map/all_gather | solution.py:102
  7.9 266.9 %all-gather.3.cloned.1.call-start = ((), (), s32[]{:S(2)}) async-start(), calls=%async_computation.3 | async-start | bytes 20971520 | tf_op jit(solution)/shard_map/all_gather | solution.py:101
  11.0 35.3 %all-to-all-start.1 = ((f32[4,2,16,2048]{3,2,1,0:T(8,128)}), f32[4,2,16,2048]{3,2,1,0:T(8,128)S(1)}, u32[]{:S(2)}, u32[]{:S(2)}) async-start(f32[4,2,16,2048]{3,2,1,0:T(8,128)} %bitcast.94), calls=%async_computation.1 | async-start | bytes 2097152 | tf_op jit(solution)/shard_map/all_to_all | solution.py:42
  29.3 16.9 %copy-start.11 = (s32[8]{0:T(128)S(1)}, s32[8]{0:T(128)}, u32[]{:S(2)}) copy-start(s32[8]{0:T(128)} %param.23) | copy-start | bytes 100
  46.3 98.3 %all-to-all-start = ((bf16[4,2,127,2048]{3,1,2,0:T(2,128)(2,1)}), bf16[4,2,127,2048]{3,1,2,0:T(2,128)(2,1)}, u32[]{:S(2)}, u32[]{:S(2)}) async-start(bf16[4,2,127,2048]{3,1,2,0:T(2,128)(2,1)} %copy.23), calls=%async_computation | async-start | bytes 8323072 | tf_op jit(solution)/shard_map/all_to_all | solution.py:41
  51.3 255.7 %reduce-scatter.2.cloned.1.call-start = ((), (), s32[]{:S(2)}) async-start(), calls=%async_computation.5 | async-start | bytes 655360 | tf_op jit(solution)/shard_map/reduce_scatter | solution.py:109
  70.0 11.6 %copy-start.7 = (f32[16,2048]{1,0:T(8,128)S(1)}, f32[16,2048]{1,0:T(8,128)}, u32[]{:S(2)}) copy-start(f32[16,2048]{1,0:T(8,128)} %param.20) | copy-start | bytes 393220
  72.0 9.6 %copy-start.3 = (f32[16,16,2048]{2,1,0:T(8,128)S(1)}, f32[16,16,2048]{2,1,0:T(8,128)}, u32[]{:S(2)}) copy-start(f32[16,16,2048]{2,1,0:T(8,128)} %gather_fusion.3) | copy-start | bytes 6291460
  150.6 7.2 %copy-start.5 = (f32[2048,127]{0,1:T(8,128)S(1)}, f32[2048,127]{0,1:T(8,128)}, u32[]{:S(2)}) copy-start(f32[2048,127]{0,1:T(8,128)} %bitcast_convert_fusion.1) | copy-start | bytes 3121156
  150.6 7.2 %copy-start.9 = (pred[16]{0:T(512)(128)(4,1)S(1)}, pred[16]{0:T(512)(128)(4,1)}, u32[]{:S(2)}) copy-start(pred[16]{0:T(512)(128)(4,1)} %get-tuple-element.8) | copy-start | bytes 52
  157.8 14.4 %copy-start.4 = (f32[2048,126]{0,1:T(8,128)S(1)}, f32[2048,126]{0,1:T(8,128)}, u32[]{:S(2)}) copy-start(f32[2048,126]{0,1:T(8,128)} %bitcast_convert_fusion) | copy-start | bytes 3096580
  168.8 3.4 %copy-start.2 = (bf16[16,127,2048]{2,0,1:T(8,128)(2,1)}, bf16[16,127,2048]{2,0,1:T(8,128)(2,1)S(1)}, u32[]{:S(2)}) copy-start(bf16[16,127,2048]{2,0,1:T(8,128)(2,1)S(1)} %get-tuple-element.6) | copy-start | bytes 24969220
  168.8 5.8 %copy-start.6 = (bf16[2,3,16,2048]{3,2,1,0:T(8,128)(2,1)S(1)}, bf16[2,3,16,2048]{3,2,1,0:T(8,128)(2,1)}, u32[]{:S(2)}) copy-start(bf16[2,3,16,2048]{3,2,1,0:T(8,128)(2,1)} %param.12) | copy-start | bytes 1179652
  274.9 9.5 %copy-start.8 = (pred[1,4,8,128]{3,1,2,0:T(4,128)(4,1)S(1)}, pred[1,4,8,128]{3,1,2,0:T(4,128)(4,1)}, u32[]{:S(2)}) copy-start(pred[1,4,8,128]{3,1,2,0:T(4,128)(4,1)} %copy.46) | copy-start | bytes 12292
  274.9 10.4 %copy-start.12 = (s32[16]{0:T(128)S(1)}, s32[16]{0:T(128)}, u32[]{:S(2)}) copy-start(s32[16]{0:T(128)} %param.17) | copy-start | bytes 196
  293.4 15.3 %copy-start.1 = (f32[16,16,2048]{2,1,0:T(8,128)S(1)}, f32[16,16,2048]{2,1,0:T(8,128)}, u32[]{:S(2)}) copy-start(f32[16,16,2048]{2,1,0:T(8,128)} %param.15) | copy-start | bytes 6291460
Sparse Core Ops, SparseCore 0:
  9.6 156.7 all-gather.4
  167.9 106.8 all-gather.2
  285.4 21.6 reduce-scatter.1
where the time goes:
time: 316 us; the launch traced here: 315 us
  waiting for transfers between devices  155 us (49%)
  local copies, waits for them, and re-layouts  81 us (26%)
  other arithmetic  36 us (11%)
  matrix products  20.1 us (6%)
  between operations  13.9 us (4%)
  starting transfers between devices  9.4 us (3%)
    all_gather x1, waiting for transfers between devices, body(): mr_piece = lax.all_gather(mr_panels, 'engine', axis=0, tiled=True)  88.8 us
    all_to_all x1, waiting for transfers between devices, body(): lax.all_to_all(send_tails, 'engine', split_axis=0, concat_axis=0, tiled=T...  58.1 us
    gather x1, local copies, waits for them, and re-layouts, body(): conv_tails[src_local]  18.6 us
    reshape x2, local copies, waits for them, and re-layouts, body(): conv_tails[send_index.reshape(-1)].reshape(engines, CAP, tail_len, width)  16.3 us
    gather x1, local copies, waits for them, and re-layouts, body(): conv_tails[send_index.reshape(-1)].reshape(engines, CAP, tail_len, width)  13.2 us
    dot_general x1, matrix products, body(): jnp.einsum('srd,gdc->srgc', li_rows, li_piece, preferred_element_type=jnp...  11.4 us
    dot_general x1, other arithmetic, body(): jnp.einsum('rtc,tc->rc', tails, mr_filter[1:], preferred_element_type=jnp...  11 us
    dot_general x1, matrix products, body(): jnp.einsum('srd,gdc->srgc', mr_rows, mr_piece, preferred_element_type=jnp...  8.7 us
  transfers between devices with their start and end apart: 5, of which 3 were waited for; matrix products, arithmetic and copies ran while one was open for 39% of the time, Pallas kernels for 0%

commit v1 on v0

--- a/solution.py
+++ b/solution.py
@@ -98,7 +98,14 @@
     )
     mr_rows = jnp.stack([ymr0, ymr1])
     li_rows = jnp.stack([yli0, yli1])
-    mr_piece = lax.all_gather(mr_panels, "engine", axis=0, tiled=True)
+    r_now, item_now = (lax.axis_size("engine"), lax.axis_index("engine"))
+    mr_piece, h_now = (mr_panels, 1)
+    while h_now < r_now:
+        work_now = lax.ppermute(mr_piece, "engine", [(j, j ^ h_now) for j in range(r_now)])
+        t1 = jnp.concatenate([mr_piece, work_now], 0)
+        y = jnp.concatenate([work_now, mr_piece], 0)
+        mr_piece = jnp.where(item_now & h_now == 0, t1, y)
+        h_now = 2 * h_now
     li_piece = lax.all_gather(li_panels, "engine", axis=0, tiled=True)
     upper = jnp.einsum("srd,gdc->srgc", mr_rows, mr_piece, preferred_element_type=jnp.float32)
     lower = jnp.einsum("srd,gdc->srgc", li_rows, li_piece, preferred_element_type=jnp.float32)

time: 316 us -> 444 us (1.41)
  waiting for transfers between devices: 155 us -> 267 us
  other arithmetic: 36 us -> 47.5 us
    all_to_all x1, waiting for transfers between devices: 0.01 us -> 241 us  [body(): lax.all_to_all(send_states, 'engine', split_axis=0, concat_axis=0, tiled=...]
    all_gather x1 -> x0, waiting for transfers between devices: 88.8 us -> none  [body(): mr_piece = lax.all_gather(mr_panels, 'engine', axis=0, tiled=True)]
    all_to_all x1, waiting for transfers between devices: 58.1 us -> 12.7 us  [body(): lax.all_to_all(send_tails, 'engine', split_axis=0, concat_axis=0, tiled=T...]
    select_n x0 -> x1, other arithmetic: none -> 11.8 us  [body(): mr_piece = jnp.where(item_now & h_now == 0, t1, y)]
    ppermute x0 -> x2, waiting for transfers between devices: none -> 5.78 us  [body(): lax.ppermute(mr_piece, 'engine', [(j, j ^ h_now) for j in range(r_now)])]
  transfers between devices with their start and end apart: 5 -> 6, of which waited for: 3 -> 4; matrix products, arithmetic and copies ran while one was open for 39% -> 29% of each run, Pallas kernels for 0% -> 0%
where the time goes in v1:
time: 444 us; the launch traced here: 443 us
  waiting for transfers between devices  267 us (60%)
  local copies, waits for them, and re-layouts  80.4 us (18%)
  other arithmetic  47.5 us (11%)
  matrix products  21.1 us (5%)
  between operations  14.2 us (3%)
  starting transfers between devices  12.5 us (3%)
    all_to_all x1, waiting for transfers between devices, body(): lax.all_to_all(send_states, 'engine', split_axis=0, concat_axis=0, tiled=...  241 us
    gather x1, local copies, waits for them, and re-layouts, body(): conv_tails[src_local]  18.4 us
    reshape x2, local copies, waits for them, and re-layouts, body(): conv_tails[send_index.reshape(-1)].reshape(engines, CAP, tail_len, width)  16.3 us
    all_to_all x1, waiting for transfers between devices, body(): lax.all_to_all(send_tails, 'engine', split_axis=0, concat_axis=0, tiled=T...  12.7 us
    dot_general x1, matrix products, body(): jnp.einsum('srd,gdc->srgc', mr_rows, mr_piece, preferred_element_type=jnp...  12.4 us
    gather x1, local copies, waits for them, and re-layouts, body(): conv_tails[send_index.reshape(-1)].reshape(engines, CAP, tail_len, width)  12.1 us
    select_n x1, other arithmetic, body(): mr_piece = jnp.where(item_now & h_now == 0, t1, y)  11.8 us
    dot_general x1, other arithmetic, body(): jnp.einsum('rtc,tc->rc', tails, mr_filter[1:], preferred_element_type=jnp...  10.8 us
  transfers between devices with their start and end apart: 6, of which 4 were waited for; matrix products, arithmetic and copies ran while one was open for 29% of the time, Pallas kernels for 0%

profile of v1, /device:TPU:0, one launch (start us, length us, event | category | flops | bytes accessed | tf_op | source)
XLA Modules:
  0.0 442.7 jit_solution(2299293335546663657)
XLA Ops:
  7.2 0.7 all-gather.2.cloned.1.call-update
  7.9 0.5 collective-permute-start
  8.4 0.7 reshape.363
  9.2 0.1 fusion.38
  9.3 0.2 reduce_window_sum.11
  9.5 0.1 select_reduce_fusion
  9.6 0.1 copy.22
  9.7 0.1 reshape.364
  9.8 5.8 %collective-permute-done = bf16[2,2048,512]{2,1,0:T(8,128)(2,1)} collective-permute-done((bf16[2,2048,512]{2,1,0:T(8,128)(2,1)}, bf16[2,2048,512]{2,1,0:T(8,128)(2,1)}, u32[]{:S(2)}, u32[]{:S(2)}) %collective-permute-start) | collective-permute-done | bytes 4194336 | tf_op jit(solution)/shard_map/ppermute | solution.py:104
  15.6 11.8 %maximum_select_fusion.1 = bf16[4,2048,512]{2,1,0:T(8,128)(2,1)} fusion(bf16[2,2048,512]{2,1,0:T(8,128)(2,1)} %collective-permute-done, bf16[2,2048,512]{2,1,0:T(8,128)(2,1)} %param.21, pred[]{:T(512)S(6)} %eq.67), kind=kLoop, calls=%fused_computation.15 | loop fusion | flops 12582912 | bytes 16777216 | tf_op jit(solution)/shard_map/jit(_where)/select_n | solution.py:107
  27.3 3.3 collective-permute-start.1
  30.7 1.6 gather_fusion.4
  32.3 3.5 all-to-all-start.1
  35.8 0.6 broadcast_compare_fusion.1
  36.4 0.2 convert_reduce_fusion
  36.6 12.1 %gather_fusion.1 = bf16[8,127,2048]{2,0,1:T(8,128)(2,1)} fusion(bf16[16,127,2048]{2,0,1:T(8,128)(2,1)} %param.14, s32[1024]{0:T(1024)S(1)} %pad_clamp_fusion.2), kind=kCustom, calls=%fused_computation.1 | custom fusion | bytes 8323104 | tf_op jit(solution)/shard_map/gather | solution.py:37
  48.7 9.2 %reshape.365 = bf16[4,2,127,2048]{3,1,0,2:T(2,128)(2,1)} reshape(bf16[8,127,2048]{2,0,1:T(8,128)(2,1)} %gather_fusion.1) | data formatting | bytes 8323072 | tf_op jit(solution)/shard_map/reshape | solution.py:37
  58.0 7.0 %copy.23 = bf16[4,2,127,2048]{3,1,2,0:T(2,128)(2,1)} copy(bf16[4,2,127,2048]{3,1,0,2:T(2,128)(2,1)} %reshape.365) | data formatting | bytes 8323072 | tf_op jit(solution)/shard_map/reshape | solution.py:37
  65.0 0.6 pad_clamp_fusion.1
  65.7 241.4 %all-to-all-done.1 = f32[4,2,16,2048]{3,2,1,0:T(8,128)S(1)} async-done(((f32[4,2,16,2048]{3,2,1,0:T(8,128)}), f32[4,2,16,2048]{3,2,1,0:T(8,128)S(1)}, u32[]{:S(2)}, u32[]{:S(2)}) %all-to-all-start.1) | async-done | bytes 1048608 | tf_op jit(solution)/shard_map/all_to_all | solution.py:42
  307.1 4.9 %all-to-all-start = ((bf16[4,2,127,2048]{3,1,2,0:T(2,128)(2,1)}), bf16[4,2,127,2048]{3,1,2,0:T(2,128)(2,1)}, u32[]{:S(2)}, u32[]{:S(2)}) async-start(bf16[4,2,127,2048]{3,1,2,0:T(2,128)(2,1)} %copy.23), calls=%async_computation | async-start | bytes 8323072 | tf_op jit(solution)/shard_map/all_to_all | solution.py:41
  311.9 0.2 reduce-scatter.2.cloned.1.call-start
  312.2 18.4 %gather_fusion = bf16[16,127,2048]{2,0,1:T(8,128)(2,1)} fusion(bf16[16,127,2048]{2,0,1:T(8,128)(2,1)} %param.14, s32[1024]{0:T(1024)S(1)} %pad_clamp_fusion.3), kind=kCustom, calls=%fused_computation | custom fusion | bytes 16646208 | tf_op jit(solution)/shard_map/gather | solution.py:53
  330.6 2.0 gather_fusion.3
  332.6 0.6 copy.46
  333.2 0.6 pad_clamp_fusion
  333.8 0.8 fusion.40
  334.7 1.0 fusion.25
  335.7 2.2 bitcast_convert_fusion.1
  337.9 2.2 bitcast_convert_fusion
  340.0 2.2 gather_fusion.5
  342.2 4.0 multiply_reduce_fusion.3
  346.2 0.9 fusion.21
  347.1 12.7 %all-to-all-done = bf16[4,2,127,2048]{3,1,2,0:T(2,128)(2,1)} async-done(((bf16[4,2,127,2048]{3,1,2,0:T(2,128)(2,1)}), bf16[4,2,127,2048]{3,1,2,0:T(2,128)(2,1)}, u32[]{:S(2)}, u32[]{:S(2)}) %all-to-all-start) | async-done | bytes 4161568 | tf_op jit(solution)/shard_map/all_to_all | solution.py:41
  359.8 6.0 %copy.24 = bf16[4,2,127,2048]{3,2,1,0:T(8,128)(2,1)} copy(bf16[4,2,127,2048]{3,1,2,0:T(2,128)(2,1)} %all-to-all-done) | data formatting | bytes 8323072 | tf_op jit(solution)/shard_map/all_to_all | solution.py:41
  365.8 7.1 %gather_fusion.2 = bf16[16,127,2048]{2,1,0:T(8,128)(2,1)} fusion(bf16[8,127,2048]{2,1,0:T(8,128)(2,1)} %bitcast.92, s32[1024]{0:T(1024)} %pad_clamp_fusion.1), kind=kCustom, calls=%fused_computation.2 | custom fusion | bytes 16646208 | tf_op jit(solution)/shard_map/gather | solution.py:54
  373.0 10.8 %multiply_reduce_fusion = (f32[2048,16]{0,1:T(8,128)S(1)}, bf16[16,127,2048]{2,0,1:T(8,128)(2,1)S(1)}) fusion(f32[2048,127]{0,1:T(8,128)S(1)} %copy-done.5, bf16[16,127,2048]{2,0,1:T(8,128)(2,1)} %gather_fusion, bf16[16,127,2048]{2,1,0:T(8,128)(2,1)} %gather_fusion.2, pred[16]{0:T(512)(128)(4,1)S(1)} %copy-done.9), kind=kLoop, calls=%fused_computation.13 | loop fusion | flops 16613376 | bytes 26140688 | tf_op jit(solution)/shard_map/rtc,tc->rc/dot_general | solution.py:62
  383.8 3.3 copy-done.2
  387.2 2.4 multiply_reduce_fusion.1
  389.6 0.1 fusion.27
  389.7 8.7 %fusion.1 = f32[2,16,8,512]{3,1,2,0:T(8,128)S(1)} fusion(bf16[8,2048,512]{2,1,0:T(8,128)(2,1)} %all-gather.2.cloned.1.call-done, bf16[1,16,2048]{2,1,0:T(8,128)(2,1)S(1)} %get-tuple-element.20, bf16[1,16,2048]{2,1,0:T(8,128)(2,1)S(1)} %get-tuple-element.19), kind=kOutput, calls=%fused_computation.9 | convolution fusion | flops 537133056 | bytes 17432576 | tf_op jit(solution)/shard_map/srd,gdc->srgc/dot_general | solution.py:111
  398.4 12.4 %fusion.6 = f32[2,16,8,512]{3,1,2,0:T(8,128)S(1)} fusion(f32[2,16,8,512]{3,1,2,0:T(8,128)S(1)} %fusion.1, bf16[4,2048,512]{2,1,0:T(8,128)(2,1)} %collective-permute-done.1, bf16[4,2048,512]{2,1,0:T(8,128)(2,1)} %maximum_select_fusion.1, pred[]{:T(512)S(6)} %eq.66, bf16[1,16,2048]{2,1,0:T(8,128)(2,1)S(1)} %get-tuple-element.16, ...), kind=kOutput, calls=%fused_computation.23 | convolution fusion | flops 612761600 | bytes 17956864 | tf_op jit(solution)/shard_map/srd,gdc->srgc/dot_general | solution.py:110
  410.8 0.7 gather_fusion.6
  411.5 0.9 broadcast_select_fusion
  412.5 8.1 %slice.90 = bf16[16,125,2048]{2,0,1:T(8,128)(2,1)} slice(bf16[16,127,2048]{2,0,1:T(8,128)(2,1)} %copy-done.2), slice={[0:16], [0:125], [0:2048]} | slice | bytes 16384000 | tf_op jit(solution)/shard_map/slice | solution.py:73
  420.6 7.2 %pad_maximum_fusion = bf16[16,127,2048]{2,0,1:T(8,128)(2,1)} fusion(bf16[16,125,2048]{2,0,1:T(8,128)(2,1)} %slice.90, bf16[16,1,2048]{2,0,1:T(8,128)(2,1)S(1)} %get-tuple-element.18, bf16[16,1,2048]{2,0,1:T(8,128)(2,1)S(1)} %get-tuple-element.17), kind=kLoop, calls=%fused_computation.16 | loop fusion | flops 8323072 | bytes 16646144 | tf_op jit(solution)/shard_map/concatenate | solution.py:72
  427.8 6.4 %reduce-scatter.2.cloned.1.call-done = f32[2,16,1024]{2,1,0:T(8,128)} async-done(((f32[2,16,4096]{2,1,0:T(8,128)}), f32[2,16,1024]{2,1,0:T(8,128)}) %reduce-scatter.2.cloned.1.call-update) | async-done | bytes 131088 | tf_op jit(solution)/shard_map/reduce_scatter | solution.py:116
  434.2 1.6 multiply_convert_fusion
  (43 shorter events, 0.4 us)
Async XLA Ops:
  7.2 23.5 %copy-start = (f32[16,16,2048]{2,1,0:T(8,128)S(1)}, f32[16,16,2048]{2,1,0:T(8,128)}, u32[]{:S(2)}) copy-start(f32[16,16,2048]{2,1,0:T(8,128)} %param.15) | copy-start | bytes 6291460
  7.2 382.5 %all-gather.2.cloned.1.call-start = ((), (), s32[]{:S(2)}) async-start(), calls=%async_computation.3 | async-start | bytes 20971520 | tf_op jit(solution)/shard_map/all_gather | solution.py:109
  7.9 7.6 %collective-permute-start = (bf16[2,2048,512]{2,1,0:T(8,128)(2,1)}, bf16[2,2048,512]{2,1,0:T(8,128)(2,1)}, u32[]{:S(2)}, u32[]{:S(2)}) collective-permute-start(bf16[2,2048,512]{2,1,0:T(8,128)(2,1)} %param.21), channel_id=1, source_target_pairs={{0,4},{4,0},{8,12},{12,8},{1,5},{5,1},{9,13},{13,9},{2,6},{6,2},{1... | collective-permute-start | bytes 12582920 | tf_op jit(solution)/shard_map/ppermute | solution.py:104
  9.8 26.0 %copy-start.10 = (s32[64]{0:T(128)S(1)}, s32[64]{0:T(128)}, u32[]{:S(2)}) copy-start(s32[64]{0:T(128)} %param.16) | copy-start | bytes 772
  27.3 371.0 %collective-permute-start.1 = (bf16[4,2048,512]{2,1,0:T(8,128)(2,1)}, bf16[4,2048,512]{2,1,0:T(8,128)(2,1)}, u32[]{:S(2)}, u32[]{:S(2)}) collective-permute-start(bf16[4,2048,512]{2,1,0:T(8,128)(2,1)} %maximum_select_fusion.1), channel_id=1, source_target_pairs={{0,8},{4,12},{8,0},{12,4},{1,9},{5,13},{9,1},{13,5},{2,10},{6,14},... | collective-permute-start | bytes 25165832 | tf_op jit(solution)/shard_map/ppermute | solution.py:104
  32.3 274.8 %all-to-all-start.1 = ((f32[4,2,16,2048]{3,2,1,0:T(8,128)}), f32[4,2,16,2048]{3,2,1,0:T(8,128)S(1)}, u32[]{:S(2)}, u32[]{:S(2)}) async-start(f32[4,2,16,2048]{3,2,1,0:T(8,128)} %bitcast.94), calls=%async_computation.1 | async-start | bytes 2097152 | tf_op jit(solution)/shard_map/all_to_all | solution.py:42
  48.7 16.9 %copy-start.11 = (s32[8]{0:T(128)S(1)}, s32[8]{0:T(128)}, u32[]{:S(2)}) copy-start(s32[8]{0:T(128)} %param.23) | copy-start | bytes 100
  307.1 52.7 %all-to-all-start = ((bf16[4,2,127,2048]{3,1,2,0:T(2,128)(2,1)}), bf16[4,2,127,2048]{3,1,2,0:T(2,128)(2,1)}, u32[]{:S(2)}, u32[]{:S(2)}) async-start(bf16[4,2,127,2048]{3,1,2,0:T(2,128)(2,1)} %copy.23), calls=%async_computation | async-start | bytes 8323072 | tf_op jit(solution)/shard_map/all_to_all | solution.py:41
  311.9 122.3 %reduce-scatter.2.cloned.1.call-start = ((), (), s32[]{:S(2)}) async-start(), calls=%async_computation.4 | async-start | bytes 655360 | tf_op jit(solution)/shard_map/reduce_scatter | solution.py:116
  330.6 11.5 %copy-start.7 = (f32[16,2048]{1,0:T(8,128)S(1)}, f32[16,2048]{1,0:T(8,128)}, u32[]{:S(2)}) copy-start(f32[16,2048]{1,0:T(8,128)} %param.20) | copy-start | bytes 393220
  332.6 9.5 %copy-start.3 = (f32[16,16,2048]{2,1,0:T(8,128)S(1)}, f32[16,16,2048]{2,1,0:T(8,128)}, u32[]{:S(2)}) copy-start(f32[16,16,2048]{2,1,0:T(8,128)} %gather_fusion.3) | copy-start | bytes 6291460
  365.8 7.1 %copy-start.5 = (f32[2048,127]{0,1:T(8,128)S(1)}, f32[2048,127]{0,1:T(8,128)}, u32[]{:S(2)}) copy-start(f32[2048,127]{0,1:T(8,128)} %bitcast_convert_fusion.1) | copy-start | bytes 3121156
  365.8 7.1 %copy-start.9 = (pred[16]{0:T(512)(128)(4,1)S(1)}, pred[16]{0:T(512)(128)(4,1)}, u32[]{:S(2)}) copy-start(pred[16]{0:T(512)(128)(4,1)} %get-tuple-element.8) | copy-start | bytes 52
  373.0 14.2 %copy-start.4 = (f32[2048,126]{0,1:T(8,128)S(1)}, f32[2048,126]{0,1:T(8,128)}, u32[]{:S(2)}) copy-start(f32[2048,126]{0,1:T(8,128)} %bitcast_convert_fusion) | copy-start | bytes 3096580
  383.8 3.4 copy-start.2
  383.8 5.8 %copy-start.6 = (bf16[2,3,16,2048]{3,2,1,0:T(8,128)(2,1)S(1)}, bf16[2,3,16,2048]{3,2,1,0:T(8,128)(2,1)}, u32[]{:S(2)}) copy-start(bf16[2,3,16,2048]{3,2,1,0:T(8,128)(2,1)} %param.12) | copy-start | bytes 1179652
  398.4 13.2 %copy-start.8 = (pred[1,4,8,128]{3,1,2,0:T(4,128)(4,1)S(1)}, pred[1,4,8,128]{3,1,2,0:T(4,128)(4,1)}, u32[]{:S(2)}) copy-start(pred[1,4,8,128]{3,1,2,0:T(4,128)(4,1)} %copy.46) | copy-start | bytes 12292
  398.4 14.1 %copy-start.12 = (s32[16]{0:T(128)S(1)}, s32[16]{0:T(128)}, u32[]{:S(2)}) copy-start(s32[16]{0:T(128)} %param.17) | copy-start | bytes 196
  420.6 15.2 %copy-start.1 = (f32[16,16,2048]{2,1,0:T(8,128)S(1)}, f32[16,16,2048]{2,1,0:T(8,128)}, u32[]{:S(2)}) copy-start(f32[16,16,2048]{2,1,0:T(8,128)} %param.15) | copy-start | bytes 6291460
Sparse Core Ops, SparseCore 0:
  9.6 192.9 all-gather.1
  412.6 21.6 reduce-scatter.1
